TPU v7x, 512 devices: a whole 4x8x8 slice. The times are simulated.
512 devices in a mesh: py: 32 (over y, x), pz: 16 (over z, core).
Axes of the slice: x: 4, y: 8, z: 8, core: 2. Of those that a mesh axis runs over, the one named last changes fastest.
Arguments:
- velocity: float32 [3, 32, 1024, 1024], P(None, 'py', 'pz'), may hold values from -14 to 14
Outputs:
- nu_t: float32 [32, 1024, 1024], P('py', 'pz')
- filtered_velocity: bfloat16 [3, 32, 1024, 1024], P(None, 'py', None, 'pz')
All inputs are finite; a program needn't handle non-finite values.
Results may differ from a plain program's by a relative error of at most 0.012.
The roundings to bfloat16 on the way count: a program that leaves them out, or rounds other values in their place, can miss the bound.
Values may be sent and summed in bfloat16 or wider, within the bound.
No kernel may reach another device: no remote copies, remote signals or barrier semaphores. Data moves between devices by JAX's collectives and lax.ppermute only.
A program may use at most 64 MiB of HBM per device.

v0:
```python
import math
import jax
import jax.numpy as jnp
import numpy as np
from jax import lax
from jax.sharding import PartitionSpec as P

index_pairs = ((0, 0), (1, 1), (2, 2), (0, 1), (0, 2), (1, 2))
pair_weights = (1.0, 1.0, 1.0, 2.0, 2.0, 2.0)
epsilon = 1e-06


def extended(x, sides, width):
    edges = {}
    for axis, dim in sides:
        devices, length = (lax.axis_size(axis), x.shape[dim])
        up = [(i, (i + 1) % devices) for i in range(devices)]
        last = lax.slice_in_dim(x, length - width, length, axis=dim)
        initial = lax.slice_in_dim(x, 0, width, axis=dim)
        edges[dim] = (
            lax.ppermute(last, axis, up),
            lax.ppermute(initial, axis, [(b, a) for a, b in up]),
        )
    done = []
    for _, dim in sides:
        low, high = edges[dim]
        around = [(width, width) if d in done else (0, 0) for d in range(x.ndim)]
        x = jnp.concatenate([jnp.pad(low, around), x, jnp.pad(high, around)], axis=dim)
        done.append(dim)
    return x


def copy_for_each(x, axis):
    copies = jnp.broadcast_to(x, (lax.axis_size(axis), *x.shape))
    return lax.all_to_all(copies, axis, split_axis=0, concat_axis=0, tiled=True)


def taken_together(x, axis):
    return copy_for_each(x, axis).sum(axis=0)


def packed_total(arrays, axis):
    line, at, gathered = (jnp.concatenate([a.reshape(-1) for a in arrays]), 0, [])
    running = taken_together(line, axis)
    for a in arrays:
        gathered.append(running[at : at + a.size].reshape(a.shape))
        at += a.size
    return tuple(gathered)


def filter_table(length):
    offsets = np.arange(length, dtype=np.int64)
    wavenumbers = np.arange(1, length // 4, dtype=np.int64)
    phase = offsets[:, None] * wavenumbers[None, :] % length
    kernel = (1.0 + 2.0 * np.cos(phase * (2.0 * math.pi / length)).sum(axis=1)) / length
    kernel = kernel.astype(np.float32)
    lagged = (offsets[:, None] - offsets[None, :]) % length
    return jnp.asarray(kernel[lagged], dtype=jnp.float32).astype(jnp.bfloat16)


def seal_walls(padded):
    device_index = lax.axis_index("py")
    last_index = lax.axis_size("py") - 1
    lower_rim = jnp.where(device_index == 0, jnp.zeros_like(padded[:, :1]), padded[:, :1])
    upper_rim = jnp.where(
        device_index == last_index, jnp.zeros_like(padded[:, -1:]), padded[:, -1:]
    )
    return jnp.concatenate([lower_rim, padded[:, 1:-1], upper_rim], axis=1)


def derivatives(padded, rim_axis):
    padded = padded.astype(jnp.float32)
    if rim_axis == 2:
        interior = padded[:, 1:-1, 1:-1, :]
        slope_rim = (padded[:, 1:-1, 2:, :] - padded[:, 1:-1, :-2, :]) * 0.5
        slope_roll = (jnp.roll(interior, -1, 3) - jnp.roll(interior, 1, 3)) * 0.5
        slope_y = (padded[:, 2:, 1:-1, :] - padded[:, :-2, 1:-1, :]) * 0.5
        return (slope_roll, slope_y, slope_rim)
    interior = padded[:, 1:-1, :, 1:-1]
    slope_rim = (padded[:, 1:-1, :, 2:] - padded[:, 1:-1, :, :-2]) * 0.5
    slope_roll = (jnp.roll(interior, -1, 2) - jnp.roll(interior, 1, 2)) * 0.5
    slope_y = (padded[:, 2:, :, 1:-1] - padded[:, :-2, :, 1:-1]) * 0.5
    return (slope_rim, slope_y, slope_roll)


def strain(gradients):
    strain_parts = [0.5 * (gradients[b][a] + gradients[a][b]) for a, b in index_pairs]
    squares_sum = pair_weights[0] * strain_parts[0] * strain_parts[0]
    for weight, part_value in zip(pair_weights[1:], strain_parts[1:]):
        squares_sum = squares_sum + weight * part_value * part_value
    return (strain_parts, jnp.sqrt(2.0 * squares_sum))


def lilly_sums(filtered, padded_hat, rim_axis):
    hat_parts, magnitude_hat = strain(derivatives(padded_hat, rim_axis))
    smooth_velocity = filtered[:3].astype(jnp.float32)
    numerator = jnp.zeros_like(magnitude_hat)
    denominator = jnp.zeros_like(magnitude_hat)
    for pair_index, (a, b) in enumerate(index_pairs):
        leonard = (
            filtered[3 + pair_index].astype(jnp.float32) - smooth_velocity[a] * smooth_velocity[b]
        )
        model_term = (
            filtered[9 + pair_index].astype(jnp.float32)
            - 4.0 * magnitude_hat * hat_parts[pair_index]
        )
        numerator = numerator + pair_weights[pair_index] * leonard * model_term
        denominator = denominator + pair_weights[pair_index] * model_term * model_term
    return (jnp.sum(numerator, axis=(1, 2)), jnp.sum(denominator, axis=(1, 2)))


def body(velocity):
    padded = extended(velocity, (("py", 1), ("pz", 2)), 1)
    strain_parts, magnitude = strain(derivatives(seal_walls(padded), 2))
    pieces = [velocity[a].astype(jnp.bfloat16) for a in range(3)]
    pieces = pieces + [(velocity[a] * velocity[b]).astype(jnp.bfloat16) for a, b in index_pairs]
    pieces = pieces + [(magnitude * part_value).astype(jnp.bfloat16) for part_value in strain_parts]
    fields = jnp.stack(pieces)
    table_x = filter_table(velocity.shape[3])
    table_z = filter_table(velocity.shape[2] * lax.axis_size("pz"))
    along_x = jnp.einsum(
        "fyzx,xv->fyzv", fields, table_x, preferred_element_type=jnp.float32
    ).astype(jnp.bfloat16)
    filtered = jnp.einsum(
        "wz,fyzx->fywx",
        table_z,
        lax.all_to_all(along_x, "pz", split_axis=3, concat_axis=2, tiled=True),
        preferred_element_type=jnp.float32,
    ).astype(jnp.bfloat16)
    padded_hat = extended(filtered[:3], (("py", 1), ("pz", 3)), 1)
    numerator, denominator = lilly_sums(filtered, seal_walls(padded_hat), 3)
    numerator, denominator = packed_total((numerator, denominator), "pz")
    plane_cells = velocity.shape[3] * velocity.shape[2] * lax.axis_size("pz")
    coefficient = numerator / plane_cells / (2.0 * (denominator / plane_cells + epsilon))
    nu_t = coefficient[:, None, None] * magnitude
    return (nu_t, filtered[:3])


def solution(mesh):
    in_specs = (P(None, "py", "pz", None),)
    out_specs = (P("py", "pz", None), P(None, "py", None, "pz"))
    return jax.shard_map(body, mesh=mesh, in_specs=in_specs, out_specs=out_specs, check_vma=False)
```

profile of v0, /device:TPU:1, one launch (start us, length us, event | category | flops | bytes accessed | tf_op | source)
XLA Modules:
  0.0 176.1 jit_solution(13759545348752628538)
XLA Ops:
  0.6 4.1 %collective-permute-start.1 = (f32[3,1,64,1024]{3,2,1,0:T(8,128)}, f32[3,1,64,1024]{3,2,1,0:T(8,128)S(1)}, u32[]{:S(2)}, u32[]{:S(2)}) collective-permute-start(f32[3,1,64,1024]{3,2,1,0:T(8,128)} %param.3), channel_id=1, source_target_pairs={{0,16},{16,32},{32,48},{48,64},{64,80},{80,96},{96,112},{112,128},... | collective-permute-start | bytes 2359304 | tf_op jit(solution)/shard_map/ppermute | solution.py:21
  4.7 6.1 %collective-permute-start.2 = (f32[3,1,64,1024]{3,2,1,0:T(8,128)}, f32[3,1,64,1024]{3,2,1,0:T(8,128)S(1)}, u32[]{:S(2)}, u32[]{:S(2)}) collective-permute-start(f32[3,1,64,1024]{3,2,1,0:T(8,128)} %param.3), channel_id=1, source_target_pairs={{16,0},{32,16},{48,32},{64,48},{80,64},{96,80},{112,96},{128,112},... | collective-permute-start | bytes 2359304 | tf_op jit(solution)/shard_map/ppermute | solution.py:22
  11.8 2.9 %collective-permute-start = (f32[3,1,1,1024]{3,2,1,0:T(1,128)S(1)}, f32[3,1,1,1024]{3,2,1,0:T(1,128)S(1)}, u32[]{:S(2)}, u32[]{:S(2)}) collective-permute-start(f32[3,1,1,1024]{3,2,1,0:T(1,128)S(1)} %get-tuple-element.24), channel_id=1, source_target_pairs={{0,1},{1,2},{2,3},{3,4},{4,5},{5,6},{6,7},{7,8},{8,9},{9,10},{10,1... | collective-permute-start | bytes 36872 | tf_op jit(solution)/shard_map/ppermute | solution.py:21
  14.7 3.1 %collective-permute-start.3 = (f32[3,1,1,1024]{3,2,1,0:T(1,128)S(1)}, f32[3,1,1,1024]{3,2,1,0:T(1,128)S(1)}, u32[]{:S(2)}, u32[]{:S(2)}) collective-permute-start(f32[3,1,1,1024]{3,2,1,0:T(1,128)S(1)} %get-tuple-element.25), channel_id=1, source_target_pairs={{1,0},{2,1},{3,2},{4,3},{5,4},{6,5},{7,6},{8,7},{9,8},{10,9},{11,1... | collective-permute-start | bytes 36872 | tf_op jit(solution)/shard_map/ppermute | solution.py:22
  23.8 1.3 copy-done.2
  26.4 1.2 copy-done.3
  28.2 1.3 copy-done.4
  29.5 3.5 %convert_bitcast_fusion = bf16[15,1,64,1024]{3,2,0,1:T(8,128)(2,1)} fusion(bf16[1024,1024,1]{1,0,2:T(8,128)(2,1)S(1)} %copy-done.4, bf16[15,1,64,1024]{3,2,0,1:T(8,128)(2,1)S(1)} %fusion.80), kind=kOutput, calls=%fused_computation.6 | convolution fusion | flops 2014248960 | bytes 6029312 | tf_op jit(solution)/shard_map/fyzx,xv->fyzv/dot_general | solution.py:121
  33.0 6.2 %copy.154 = bf16[15,1,64,1024]{2,0,1,3:T(8,128)(2,1)} copy(bf16[15,1,64,1024]{3,2,0,1:T(8,128)(2,1)} %convert_bitcast_fusion) | data formatting | bytes 3932160 | tf_op jit(solution)/shard_map/convert_element_type | solution.py:123
  39.2 7.3 %reshape.1162 = bf16[16,2,30720]{2,1,0:T(2,128)(2,1)} reshape(bf16[1024,1,15,64]{3,2,1,0:T(8,128)(2,1)} %bitcast.264) | data formatting | bytes 3932160
  46.5 61.5 %all_to_all.21 = bf16[16,2,30720]{2,1,0:T(2,128)(2,1)} all-to-all(bf16[16,2,30720]{2,1,0:T(2,128)(2,1)} %reshape.1162), channel_id=1, replica_groups=mesh['py'=32,'pz'=16] {'pz'}, dimensions={0} | all-to-all | bytes 3932160 | tf_op jit(solution)/shard_map/all_to_all | solution.py:127
  108.0 7.5 %reshape.1163 = bf16[1024,1,15,64]{3,2,1,0:T(8,128)(2,1)} reshape(bf16[16,2,30720]{2,1,0:T(2,128)(2,1)} %all_to_all.21) | data formatting | bytes 3932160
  115.5 5.8 %copy.155 = bf16[15,1,64,1024]{3,2,0,1:T(8,128)(2,1)} copy(bf16[15,1,64,1024]{2,0,1,3:T(8,128)(2,1)} %bitcast.265) | data formatting | bytes 3932160 | tf_op jit(solution)/shard_map/all_to_all | solution.py:127
  121.2 6.1 %reshape.1156 = bf16[15,1024,64]{2,1,0:T(8,128)(2,1)} reshape(bf16[15,1,64,1024]{3,2,0,1:T(8,128)(2,1)} %copy.155) | data formatting | bytes 3932160 | tf_op jit(solution)/shard_map/wz,fyzx->fywx/dot_general | solution.py:124
  127.3 7.0 %convolution_convert_fusion = bf16[15,64,1024]{2,1,0:T(8,128)(2,1)S(1)} fusion(bf16[15,1024,64]{2,1,0:T(8,128)(2,1)} %reshape.1156, bf16[1024,1024,1]{1,0,2:T(8,128)(2,1)} %constant.58), kind=kOutput, calls=%fused_computation.7 | convolution fusion | flops 2014248960 | bytes 6029312 | tf_op jit(solution)/shard_map/wz,fyzx->fywx/dot_general | solution.py:124
  134.4 7.3 %collective-permute-start.6 = (bf16[3,1,1024,64]{2,3,1,0:T(8,128)(2,1)S(1)}, bf16[3,1,1024,64]{2,3,1,0:T(8,128)(2,1)S(1)}, u32[]{:S(2)}, u32[]{:S(2)}) collective-permute-start(bf16[3,1,1024,64]{2,3,1,0:T(8,128)(2,1)S(1)} %get-tuple-element.8), channel_id=1, source_target_pairs={{16,0},{32,16},{48,32},{64,48},{80,64},{96,80},{112,96},{128,112},... | collective-permute-start | bytes 1179656 | tf_op jit(solution)/shard_map/ppermute | solution.py:22
  141.8 1.9 %collective-permute-start.5 = (bf16[3,1,1024,64]{2,3,1,0:T(8,128)(2,1)S(1)}, bf16[3,1,1024,64]{2,3,1,0:T(8,128)(2,1)S(1)}, u32[]{:S(2)}, u32[]{:S(2)}) collective-permute-start(bf16[3,1,1024,64]{2,3,1,0:T(8,128)(2,1)S(1)} %get-tuple-element.8), channel_id=1, source_target_pairs={{0,16},{16,32},{32,48},{48,64},{64,80},{80,96},{96,112},{112,128},... | collective-permute-start | bytes 1179656 | tf_op jit(solution)/shard_map/ppermute | solution.py:21
  144.9 2.3 %collective-permute-done.7 = bf16[3,1,1024,1]{2,3,1,0:T(2,128)(2,1)S(1)} collective-permute-done((bf16[3,1,1024,1]{2,3,1,0:T(2,128)(2,1)S(1)}, bf16[3,1,1024,1]{2,3,1,0:T(2,128)(2,1)S(1)}, u32[]{:S(2)}, u32[]{:S(2)}) %collective-permute-start.7) | collective-permute-done | bytes 6176 | tf_op jit(solution)/shard_map/ppermute | solution.py:22
  147.2 3.2 %collective-permute-done.6 = bf16[3,1,1024,64]{2,3,1,0:T(8,128)(2,1)S(1)} collective-permute-done((bf16[3,1,1024,64]{2,3,1,0:T(8,128)(2,1)S(1)}, bf16[3,1,1024,64]{2,3,1,0:T(8,128)(2,1)S(1)}, u32[]{:S(2)}, u32[]{:S(2)}) %collective-permute-start.6) | collective-permute-done | bytes 393248 | tf_op jit(solution)/shard_map/ppermute | solution.py:22
  150.4 7.7 %collective-permute-done.5 = bf16[3,1,1024,64]{2,3,1,0:T(8,128)(2,1)S(1)} collective-permute-done((bf16[3,1,1024,64]{2,3,1,0:T(8,128)(2,1)S(1)}, bf16[3,1,1024,64]{2,3,1,0:T(8,128)(2,1)S(1)}, u32[]{:S(2)}, u32[]{:S(2)}) %collective-permute-start.5) | collective-permute-done | bytes 393248 | tf_op jit(solution)/shard_map/ppermute | solution.py:21
  159.9 1.4 fusion.59
  162.1 1.3 pad_maximum_fusion.6
  163.4 9.8 %all_to_all.22 = f32[16,1,2]{2,1,0:T(1,128)S(1)} all-to-all(f32[16,1,2]{2,1,0:T(1,128)S(1)} %broadcast_in_dim.4), channel_id=1, replica_groups=mesh['py'=32,'pz'=16] {'pz'}, dimensions={0} | all-to-all | bytes 256 | tf_op jit(solution)/shard_map/all_to_all | solution.py:35
  175.1 1.0 fusion.44
  (51 shorter events, 13.2 us)
Async XLA Ops:
  0.6 23.0 %copy-start = (f32[3,1,64,1024]{3,2,1,0:T(8,128)S(1)}, f32[3,1,64,1024]{3,2,1,0:T(8,128)}, u32[]{:S(2)}) copy-start(f32[3,1,64,1024]{3,2,1,0:T(8,128)} %param.3) | copy-start | bytes 2359300
  0.6 25.3 %collective-permute-start.1 = (f32[3,1,64,1024]{3,2,1,0:T(8,128)}, f32[3,1,64,1024]{3,2,1,0:T(8,128)S(1)}, u32[]{:S(2)}, u32[]{:S(2)}) collective-permute-start(f32[3,1,64,1024]{3,2,1,0:T(8,128)} %param.3), channel_id=1, source_target_pairs={{0,16},{16,32},{32,48},{48,64},{64,80},{80,96},{96,112},{112,128},... | collective-permute-start | bytes 2359304 | tf_op jit(solution)/shard_map/ppermute | solution.py:21
  4.7 21.3 %collective-permute-start.2 = (f32[3,1,64,1024]{3,2,1,0:T(8,128)}, f32[3,1,64,1024]{3,2,1,0:T(8,128)S(1)}, u32[]{:S(2)}, u32[]{:S(2)}) collective-permute-start(f32[3,1,64,1024]{3,2,1,0:T(8,128)} %param.3), channel_id=1, source_target_pairs={{16,0},{32,16},{48,32},{64,48},{80,64},{96,80},{112,96},{128,112},... | collective-permute-start | bytes 2359304 | tf_op jit(solution)/shard_map/ppermute | solution.py:22
  11.8 14.1 %collective-permute-start = (f32[3,1,1,1024]{3,2,1,0:T(1,128)S(1)}, f32[3,1,1,1024]{3,2,1,0:T(1,128)S(1)}, u32[]{:S(2)}, u32[]{:S(2)}) collective-permute-start(f32[3,1,1,1024]{3,2,1,0:T(1,128)S(1)} %get-tuple-element.24), channel_id=1, source_target_pairs={{0,1},{1,2},{2,3},{3,4},{4,5},{5,6},{6,7},{7,8},{8,9},{9,10},{10,1... | collective-permute-start | bytes 36872 | tf_op jit(solution)/shard_map/ppermute | solution.py:21
  14.7 11.1 %collective-permute-start.3 = (f32[3,1,1,1024]{3,2,1,0:T(1,128)S(1)}, f32[3,1,1,1024]{3,2,1,0:T(1,128)S(1)}, u32[]{:S(2)}, u32[]{:S(2)}) collective-permute-start(f32[3,1,1,1024]{3,2,1,0:T(1,128)S(1)} %get-tuple-element.25), channel_id=1, source_target_pairs={{1,0},{2,1},{3,2},{4,3},{5,4},{6,5},{7,6},{8,7},{9,8},{10,9},{11,1... | collective-permute-start | bytes 36872 | tf_op jit(solution)/shard_map/ppermute | solution.py:22
  23.8 1.3 copy-start.2
  26.1 1.5 copy-start.3
  27.9 1.6 copy-start.4
  134.4 24.2 %copy-start.1 = (bf16[3,1,1024,64]{2,3,1,0:T(8,128)(2,1)}, bf16[3,1,1024,64]{2,3,1,0:T(8,128)(2,1)S(1)}, u32[]{:S(2)}) copy-start(bf16[3,1,1024,64]{2,3,1,0:T(8,128)(2,1)S(1)} %get-tuple-element.8) | copy-start | bytes 1179652
  134.4 16.0 %collective-permute-start.6 = (bf16[3,1,1024,64]{2,3,1,0:T(8,128)(2,1)S(1)}, bf16[3,1,1024,64]{2,3,1,0:T(8,128)(2,1)S(1)}, u32[]{:S(2)}, u32[]{:S(2)}) collective-permute-start(bf16[3,1,1024,64]{2,3,1,0:T(8,128)(2,1)S(1)} %get-tuple-element.8), channel_id=1, source_target_pairs={{16,0},{32,16},{48,32},{64,48},{80,64},{96,80},{112,96},{128,112},... | collective-permute-start | bytes 1179656 | tf_op jit(solution)/shard_map/ppermute | solution.py:22
  141.8 16.3 %collective-permute-start.5 = (bf16[3,1,1024,64]{2,3,1,0:T(8,128)(2,1)S(1)}, bf16[3,1,1024,64]{2,3,1,0:T(8,128)(2,1)S(1)}, u32[]{:S(2)}, u32[]{:S(2)}) collective-permute-start(bf16[3,1,1024,64]{2,3,1,0:T(8,128)(2,1)S(1)} %get-tuple-element.8), channel_id=1, source_target_pairs={{0,16},{16,32},{32,48},{48,64},{64,80},{80,96},{96,112},{112,128},... | collective-permute-start | bytes 1179656 | tf_op jit(solution)/shard_map/ppermute | solution.py:21
  143.7 1.2 collective-permute-start.4
  143.8 3.4 %collective-permute-start.7 = (bf16[3,1,1024,1]{2,3,1,0:T(2,128)(2,1)S(1)}, bf16[3,1,1024,1]{2,3,1,0:T(2,128)(2,1)S(1)}, u32[]{:S(2)}, u32[]{:S(2)}) collective-permute-start(bf16[3,1,1024,1]{2,3,1,0:T(2,128)(2,1)S(1)} %get-tuple-element.18), channel_id=1, source_target_pairs={{1,0},{2,1},{3,2},{4,3},{5,4},{6,5},{7,6},{8,7},{9,8},{10,9},{11,1... | collective-permute-start | bytes 18440 | tf_op jit(solution)/shard_map/ppermute | solution.py:22
where the time goes:
time: 177 us; the launch traced here: 176 us
  blocking collectives  71.3 us (40%)
  local copies, waits for them, and re-layouts  42 us (24%)
  starting transfers between devices  26 us (15%)
  waiting for transfers between devices  13.9 us (8%)
  matrix products  10.5 us (6%)
  other arithmetic  10.2 us (6%)
  between operations  2.21 us (1%)
    all_to_all x1, blocking collectives, body(): lax.all_to_all(along_x, 'pz', split_axis=3, concat_axis=2, tiled=True)  61.5 us
    unnamed x17, local copies, waits for them, and re-layouts  21.6 us
    ppermute x4, starting transfers between devices, extended(): lax.ppermute(initial, axis, [(b, a) for a, b in up])  17 us
    all_to_all x1, blocking collectives, copy_for_each(): return lax.all_to_all(copies, axis, split_axis=0, concat_axis=0, tiled=True)  9.84 us
    ppermute x4, starting transfers between devices, extended(): lax.ppermute(last, axis, up)  8.97 us
    ppermute x4, waiting for transfers between devices, extended(): lax.ppermute(last, axis, up)  8.38 us
    dot_general x1, matrix products, body(): jnp.einsum('wz,fyzx->fywx', table_z, lax.all_to_all(along_x, 'pz', split_...  7.04 us
    convert_element_type x1, local copies, waits for them, and re-layouts, body(): along_x = jnp.einsum('fyzx,xv->fyzv', fields, table_x, preferred_element_...  6.18 us
  transfers between devices with their start and end apart: 8, of which 4 were waited for; matrix products, arithmetic and copies ran while one was open for 4% of the time, Pallas kernels for 0%

commit v1 on v0

--- a/solution.py
+++ b/solution.py
@@ -124,7 +124,10 @@
     filtered = jnp.einsum(
         "wz,fyzx->fywx",
         table_z,
-        lax.all_to_all(along_x, "pz", split_axis=3, concat_axis=2, tiled=True),
+        jnp.concatenate(
+            lax.all_to_all(jnp.stack(jnp.split(along_x, lax.axis_size("pz"), axis=3)), "pz", 0, 0),
+            axis=2,
+        ),
         preferred_element_type=jnp.float32,
     ).astype(jnp.bfloat16)
     padded_hat = extended(filtered[:3], (("py", 1), ("pz", 3)), 1)

time: 177 us -> 177 us (level)
  local copies, waits for them, and re-layouts: 42 us -> 46.5 us
  matrix products: 10.5 us -> 6.6 us
    reshape x0 -> x2, local copies, waits for them, and re-layouts: none -> 11.6 us  [body(): jnp.concatenate(lax.all_to_all(jnp.stack(jnp.split(along_x, lax.axis_size...]
    another operation x0 -> x2, local copies, waits for them, and re-layouts: none -> 6.39 us
    convert_element_type x1 -> x0, local copies, waits for them, and re-layouts: 6.18 us -> none  [body(): along_x = jnp.einsum('fyzx,xv->fyzv', fields, table_x, preferred_element_...]
    dot_general x1 -> x0, local copies, waits for them, and re-layouts: 6.05 us -> none  [body(): jnp.einsum('wz,fyzx->fywx', table_z, lax.all_to_all(along_x, 'pz', split_...]
    all_to_all x1 -> x0, local copies, waits for them, and re-layouts: 5.76 us -> none  [body(): lax.all_to_all(along_x, 'pz', split_axis=3, concat_axis=2, tiled=True)]
    unnamed x17 -> x34, local copies, waits for them, and re-layouts: 21.6 us -> 26.2 us
    dot_general x1, matrix products: 7.04 us -> 4.41 us  [body(): jnp.einsum('wz,fyzx->fywx', table_z, jnp.concatenate(lax.all_to_all(jnp.s...]
  transfers between devices with their start and end apart: 8 -> 8, of which waited for: 4 -> 4; matrix products, arithmetic and copies ran while one was open for 4% -> 5% of each run, Pallas kernels for 0% -> 0%
where the time goes in v1:
time: 177 us; the launch traced here: 176 us
  blocking collectives  70.3 us (40%)
  local copies, waits for them, and re-layouts  46.5 us (26%)
  starting transfers between devices  25.9 us (15%)
  waiting for transfers between devices  13.9 us (8%)
  other arithmetic  10.4 us (6%)
  matrix products  6.6 us (4%)
  between operations  2.49 us (1%)
    all_to_all x1, blocking collectives, body(): lax.all_to_all(jnp.stack(jnp.split(along_x, lax.axis_size('pz'), axis=3))...  60.4 us
    unnamed x34, local copies, waits for them, and re-layouts  26.2 us
    ppermute x4, starting transfers between devices, extended(): lax.ppermute(initial, axis, [(b, a) for a, b in up])  16.9 us
    reshape x2, local copies, waits for them, and re-layouts, body(): jnp.concatenate(lax.all_to_all(jnp.stack(jnp.split(along_x, lax.axis_size...  11.6 us
    all_to_all x1, blocking collectives, copy_for_each(): return lax.all_to_all(copies, axis, split_axis=0, concat_axis=0, tiled=True)  9.84 us
    ppermute x4, starting transfers between devices, extended(): lax.ppermute(last, axis, up)  8.97 us
    ppermute x4, waiting for transfers between devices, extended(): lax.ppermute(last, axis, up)  8.37 us
    another operation x1, local copies, waits for them, and re-layouts  6.22 us
  transfers between devices with their start and end apart: 8, of which 4 were waited for; matrix products, arithmetic and copies ran while one was open for 5% of the time, Pallas kernels for 0%

profile of v1, /device:TPU:1, one launch (start us, length us, event | category | flops | bytes accessed | tf_op | source)
XLA Modules:
  0.0 176.1 jit_solution(1779147420500811692)
XLA Ops:
  0.6 4.1 %collective-permute-start.1 = (f32[3,1,64,1024]{3,2,1,0:T(8,128)}, f32[3,1,64,1024]{3,2,1,0:T(8,128)}, u32[]{:S(2)}, u32[]{:S(2)}) collective-permute-start(f32[3,1,64,1024]{3,2,1,0:T(8,128)} %param.3), channel_id=1, source_target_pairs={{0,16},{16,32},{32,48},{48,64},{64,80},{80,96},{96,112},{112,128},... | collective-permute-start | bytes 2359304 | tf_op jit(solution)/shard_map/ppermute | solution.py:21
  4.7 6.1 %collective-permute-start.2 = (f32[3,1,64,1024]{3,2,1,0:T(8,128)}, f32[3,1,64,1024]{3,2,1,0:T(8,128)S(1)}, u32[]{:S(2)}, u32[]{:S(2)}) collective-permute-start(f32[3,1,64,1024]{3,2,1,0:T(8,128)} %param.3), channel_id=1, source_target_pairs={{16,0},{32,16},{48,32},{64,48},{80,64},{96,80},{112,96},{128,112},... | collective-permute-start | bytes 2359304 | tf_op jit(solution)/shard_map/ppermute | solution.py:22
  11.8 2.9 %collective-permute-start = (f32[3,1,1,1024]{3,2,1,0:T(1,128)S(1)}, f32[3,1,1,1024]{3,2,1,0:T(1,128)S(1)}, u32[]{:S(2)}, u32[]{:S(2)}) collective-permute-start(f32[3,1,1,1024]{3,2,1,0:T(1,128)S(1)} %get-tuple-element.24), channel_id=1, source_target_pairs={{0,1},{1,2},{2,3},{3,4},{4,5},{5,6},{6,7},{7,8},{8,9},{9,10},{10,1... | collective-permute-start | bytes 36872 | tf_op jit(solution)/shard_map/ppermute | solution.py:21
  14.7 3.1 %collective-permute-start.3 = (f32[3,1,1,1024]{3,2,1,0:T(1,128)S(1)}, f32[3,1,1,1024]{3,2,1,0:T(1,128)S(1)}, u32[]{:S(2)}, u32[]{:S(2)}) collective-permute-start(f32[3,1,1,1024]{3,2,1,0:T(1,128)S(1)} %get-tuple-element.25), channel_id=1, source_target_pairs={{1,0},{2,1},{3,2},{4,3},{5,4},{6,5},{7,6},{8,7},{9,8},{10,9},{11,1... | collective-permute-start | bytes 36872 | tf_op jit(solution)/shard_map/ppermute | solution.py:22
  23.8 1.3 copy-done.3
  27.6 1.2 copy-done.4
  29.3 1.3 copy-done.5
  30.7 2.2 %convert_bitcast_fusion = bf16[15,1,64,1024]{3,2,0,1:T(8,128)(2,1)S(1)} fusion(bf16[1024,1024,1]{1,0,2:T(8,128)(2,1)S(1)} %copy-done.5, bf16[15,1,64,1024]{3,2,0,1:T(8,128)(2,1)S(1)} %fusion.96), kind=kOutput, calls=%fused_computation.6 | convolution fusion | flops 2014248960 | bytes 6029312 | tf_op jit(solution)/shard_map/fyzx,xv->fyzv/dot_general | solution.py:121
  35.1 1.8 %copy-done.1 = bf16[16,15,1,64,64]{4,3,1,2,0:T(8,128)(2,1)} copy-done((bf16[16,15,1,64,64]{4,3,1,2,0:T(8,128)(2,1)}, bf16[16,15,1,64,64]{4,3,1,2,0:T(8,128)(2,1)S(1)}, u32[]{:S(2)}) %copy-start.1) | copy-done | bytes 1966104
  36.9 7.2 %reshape.1162 = bf16[16,2,30720]{2,1,0:T(2,128)(2,1)} reshape(bf16[16,1,15,64,64]{4,3,2,1,0:T(8,128)(2,1)} %bitcast.330) | data formatting | bytes 3932160
  44.1 60.4 %all_to_all.11 = bf16[16,2,30720]{2,1,0:T(2,128)(2,1)} all-to-all(bf16[16,2,30720]{2,1,0:T(2,128)(2,1)} %reshape.1162), channel_id=1, replica_groups=mesh['py'=32,'pz'=16] {'pz'}, dimensions={0} | all-to-all | bytes 3932160 | tf_op jit(solution)/shard_map/all_to_all | solution.py:128
  104.5 7.3 %reshape.1163 = bf16[16,1,15,64,64]{4,3,2,1,0:T(8,128)(2,1)} reshape(bf16[16,2,30720]{2,1,0:T(2,128)(2,1)} %all_to_all.11) | data formatting | bytes 3932160
  111.8 5.0 %bitcast_bitcast_fusion = bf16[15,1,16,64,64]{4,3,0,1,2:T(8,128)(2,1)} fusion(bf16[16,1,15,64,64]{4,3,2,1,0:T(8,128)(2,1)} %reshape.1163), kind=kLoop, calls=%fused_computation.201 | loop fusion | bytes 3932160 | tf_op jit(solution)/shard_map/reshape | solution.py:127
  116.8 6.6 %copy.117 = bf16[15,1,16,64,64]{3,2,4,0,1:T(8,128)(2,1)} copy(bf16[15,1,16,64,64]{4,3,0,1,2:T(8,128)(2,1)} %bitcast_bitcast_fusion) | data formatting | bytes 3932160 | tf_op jit(solution)/shard_map/reshape | solution.py:127
  123.4 6.2 %reshape.1153 = bf16[15,1024,64]{1,2,0:T(8,128)(2,1)} reshape(bf16[15,1,16,64,64]{3,2,4,0,1:T(8,128)(2,1)} %copy.117) | data formatting | bytes 3932160 | tf_op jit(solution)/shard_map/reshape.4
  129.6 4.4 %convolution_convert_fusion = bf16[15,64,1024]{2,1,0:T(8,128)(2,1)S(1)} fusion(bf16[15,1024,64]{1,2,0:T(8,128)(2,1)} %reshape.1153, bf16[1024,1024,1]{1,0,2:T(8,128)(2,1)} %constant.54), kind=kOutput, calls=%fused_computation.7 | convolution fusion | flops 2014248960 | bytes 6029312 | tf_op jit(solution)/shard_map/wz,fyzx->fywx/dot_general | solution.py:124
  134.1 7.2 %collective-permute-start.6 = (bf16[3,1,1024,64]{2,3,1,0:T(8,128)(2,1)S(1)}, bf16[3,1,1024,64]{2,3,1,0:T(8,128)(2,1)S(1)}, u32[]{:S(2)}, u32[]{:S(2)}) collective-permute-start(bf16[3,1,1024,64]{2,3,1,0:T(8,128)(2,1)S(1)} %get-tuple-element.8), channel_id=1, source_target_pairs={{16,0},{32,16},{48,32},{64,48},{80,64},{96,80},{112,96},{128,112},... | collective-permute-start | bytes 1179656 | tf_op jit(solution)/shard_map/ppermute | solution.py:22
  141.4 1.9 %collective-permute-start.5 = (bf16[3,1,1024,64]{2,3,1,0:T(8,128)(2,1)S(1)}, bf16[3,1,1024,64]{2,3,1,0:T(8,128)(2,1)S(1)}, u32[]{:S(2)}, u32[]{:S(2)}) collective-permute-start(bf16[3,1,1024,64]{2,3,1,0:T(8,128)(2,1)S(1)} %get-tuple-element.8), channel_id=1, source_target_pairs={{0,16},{16,32},{32,48},{48,64},{64,80},{80,96},{96,112},{112,128},... | collective-permute-start | bytes 1179656 | tf_op jit(solution)/shard_map/ppermute | solution.py:21
  144.5 2.3 %collective-permute-done.7 = bf16[3,1,1024,1]{2,3,1,0:T(2,128)(2,1)S(1)} collective-permute-done((bf16[3,1,1024,1]{2,3,1,0:T(2,128)(2,1)S(1)}, bf16[3,1,1024,1]{2,3,1,0:T(2,128)(2,1)S(1)}, u32[]{:S(2)}, u32[]{:S(2)}) %collective-permute-start.7) | collective-permute-done | bytes 6176 | tf_op jit(solution)/shard_map/ppermute | solution.py:22
  146.8 3.2 %collective-permute-done.6 = bf16[3,1,1024,64]{2,3,1,0:T(8,128)(2,1)S(1)} collective-permute-done((bf16[3,1,1024,64]{2,3,1,0:T(8,128)(2,1)S(1)}, bf16[3,1,1024,64]{2,3,1,0:T(8,128)(2,1)S(1)}, u32[]{:S(2)}, u32[]{:S(2)}) %collective-permute-start.6) | collective-permute-done | bytes 393248 | tf_op jit(solution)/shard_map/ppermute | solution.py:22
  150.0 7.7 %collective-permute-done.5 = bf16[3,1,1024,64]{2,3,1,0:T(8,128)(2,1)S(1)} collective-permute-done((bf16[3,1,1024,64]{2,3,1,0:T(8,128)(2,1)S(1)}, bf16[3,1,1024,64]{2,3,1,0:T(8,128)(2,1)S(1)}, u32[]{:S(2)}, u32[]{:S(2)}) %collective-permute-start.5) | collective-permute-done | bytes 393248 | tf_op jit(solution)/shard_map/ppermute | solution.py:21
  159.5 1.4 fusion.59
  161.8 1.4 pad_maximum_fusion.6
  163.2 9.8 %all_to_all.12 = f32[16,1,2]{2,1,0:T(1,128)S(1)} all-to-all(f32[16,1,2]{2,1,0:T(1,128)S(1)} %broadcast_in_dim.4), channel_id=1, replica_groups=mesh['py'=32,'pz'=16] {'pz'}, dimensions={0} | all-to-all | bytes 256 | tf_op jit(solution)/shard_map/all_to_all | solution.py:35
  (69 shorter events, 17.5 us)
Async XLA Ops:
  0.6 23.0 %copy-start = (f32[3,1,64,1024]{3,2,1,0:T(8,128)S(1)}, f32[3,1,64,1024]{3,2,1,0:T(8,128)}, u32[]{:S(2)}) copy-start(f32[3,1,64,1024]{3,2,1,0:T(8,128)} %param.3) | copy-start | bytes 2359300
  0.6 25.2 %collective-permute-start.1 = (f32[3,1,64,1024]{3,2,1,0:T(8,128)}, f32[3,1,64,1024]{3,2,1,0:T(8,128)}, u32[]{:S(2)}, u32[]{:S(2)}) collective-permute-start(f32[3,1,64,1024]{3,2,1,0:T(8,128)} %param.3), channel_id=1, source_target_pairs={{0,16},{16,32},{32,48},{48,64},{64,80},{80,96},{96,112},{112,128},... | collective-permute-start | bytes 2359304 | tf_op jit(solution)/shard_map/ppermute | solution.py:21
  4.7 22.4 %collective-permute-start.2 = (f32[3,1,64,1024]{3,2,1,0:T(8,128)}, f32[3,1,64,1024]{3,2,1,0:T(8,128)S(1)}, u32[]{:S(2)}, u32[]{:S(2)}) collective-permute-start(f32[3,1,64,1024]{3,2,1,0:T(8,128)} %param.3), channel_id=1, source_target_pairs={{16,0},{32,16},{48,32},{64,48},{80,64},{96,80},{112,96},{128,112},... | collective-permute-start | bytes 2359304 | tf_op jit(solution)/shard_map/ppermute | solution.py:22
  11.8 14.0 %collective-permute-start = (f32[3,1,1,1024]{3,2,1,0:T(1,128)S(1)}, f32[3,1,1,1024]{3,2,1,0:T(1,128)S(1)}, u32[]{:S(2)}, u32[]{:S(2)}) collective-permute-start(f32[3,1,1,1024]{3,2,1,0:T(1,128)S(1)} %get-tuple-element.24), channel_id=1, source_target_pairs={{0,1},{1,2},{2,3},{3,4},{4,5},{5,6},{6,7},{7,8},{8,9},{9,10},{10,1... | collective-permute-start | bytes 36872 | tf_op jit(solution)/shard_map/ppermute | solution.py:21
  14.7 11.1 %collective-permute-start.3 = (f32[3,1,1,1024]{3,2,1,0:T(1,128)S(1)}, f32[3,1,1,1024]{3,2,1,0:T(1,128)S(1)}, u32[]{:S(2)}, u32[]{:S(2)}) collective-permute-start(f32[3,1,1,1024]{3,2,1,0:T(1,128)S(1)} %get-tuple-element.25), channel_id=1, source_target_pairs={{1,0},{2,1},{3,2},{4,3},{5,4},{6,5},{7,6},{8,7},{9,8},{10,9},{11,1... | collective-permute-start | bytes 36872 | tf_op jit(solution)/shard_map/ppermute | solution.py:22
  23.8 1.3 copy-start.3
  27.2 1.5 copy-start.4
  29.1 1.6 copy-start.5
  35.1 1.9 %copy-start.1 = (bf16[16,15,1,64,64]{4,3,1,2,0:T(8,128)(2,1)}, bf16[16,15,1,64,64]{4,3,1,2,0:T(8,128)(2,1)S(1)}, u32[]{:S(2)}) copy-start(bf16[16,15,1,64,64]{4,3,1,2,0:T(8,128)(2,1)S(1)} %fusion.66) | copy-start | bytes 5898244
  134.1 24.1 %copy-start.2 = (bf16[3,1,1024,64]{2,3,1,0:T(8,128)(2,1)}, bf16[3,1,1024,64]{2,3,1,0:T(8,128)(2,1)S(1)}, u32[]{:S(2)}) copy-start(bf16[3,1,1024,64]{2,3,1,0:T(8,128)(2,1)S(1)} %get-tuple-element.8) | copy-start | bytes 1179652
  134.1 15.9 %collective-permute-start.6 = (bf16[3,1,1024,64]{2,3,1,0:T(8,128)(2,1)S(1)}, bf16[3,1,1024,64]{2,3,1,0:T(8,128)(2,1)S(1)}, u32[]{:S(2)}, u32[]{:S(2)}) collective-permute-start(bf16[3,1,1024,64]{2,3,1,0:T(8,128)(2,1)S(1)} %get-tuple-element.8), channel_id=1, source_target_pairs={{16,0},{32,16},{48,32},{64,48},{80,64},{96,80},{112,96},{128,112},... | collective-permute-start | bytes 1179656 | tf_op jit(solution)/shard_map/ppermute | solution.py:22
  141.4 16.3 %collective-permute-start.5 = (bf16[3,1,1024,64]{2,3,1,0:T(8,128)(2,1)S(1)}, bf16[3,1,1024,64]{2,3,1,0:T(8,128)(2,1)S(1)}, u32[]{:S(2)}, u32[]{:S(2)}) collective-permute-start(bf16[3,1,1024,64]{2,3,1,0:T(8,128)(2,1)S(1)} %get-tuple-element.8), channel_id=1, source_target_pairs={{0,16},{16,32},{32,48},{48,64},{64,80},{80,96},{96,112},{112,128},... | collective-permute-start | bytes 1179656 | tf_op jit(solution)/shard_map/ppermute | solution.py:21
  143.3 1.2 collective-permute-start.4
  143.4 3.4 %collective-permute-start.7 = (bf16[3,1,1024,1]{2,3,1,0:T(2,128)(2,1)S(1)}, bf16[3,1,1024,1]{2,3,1,0:T(2,128)(2,1)S(1)}, u32[]{:S(2)}, u32[]{:S(2)}) collective-permute-start(bf16[3,1,1024,1]{2,3,1,0:T(2,128)(2,1)S(1)} %get-tuple-element.18), channel_id=1, source_target_pairs={{1,0},{2,1},{3,2},{4,3},{5,4},{6,5},{7,6},{8,7},{9,8},{10,9},{11,1... | collective-permute-start | bytes 18440 | tf_op jit(solution)/shard_map/ppermute | solution.py:22
